TPU v7x, 128 devices: a whole 4x4x4 slice. The times are simulated.
128 devices in a mesh: seq: 64 (over z, x, y_hi, core), ch: 2 (over y_lo).
Axes of the slice: x: 4, y: 4 (y_hi: 2, y_lo: 2; y = y_hi * 2 + y_lo), z: 4, core: 2. Of those that a mesh axis runs over, the one named last changes fastest.
Arguments:
- inputs: bfloat16 [2, 65536, 1536], P(None, 'seq', 'ch'), may hold values from -6 to 6
- cotangent: bfloat16 [2, 65536, 1536], P(None, 'seq', 'ch'), may hold values from -6 to 6
- conv_out: bfloat16 [2, 65536, 768], P(None, 'seq'), may hold values from -6 to 6
- conv_weight: bfloat16 [3, 1536, 768], P(None, 'ch'), may hold values from -0.09375 to 0.09375
- proj_weight: bfloat16 [768, 1536], P(None, 'ch'), may hold values from -0.21875 to 0.21875
Outputs:
- grad_inputs: bfloat16 [2, 65536, 1536], P(None, 'seq', 'ch')
- grad_conv: bfloat16 [3, 1536, 768], P(None, 'ch')
- grad_proj: bfloat16 [768, 1536], P(None, 'ch')
All inputs are finite; a program needn't handle non-finite values.
Results may differ from a plain program's by a relative error of at most 0.0061.
Values may be sent and summed in bfloat16 or wider, within the bound.
A program may use at most 128 MiB of HBM per device.

v0:
```python
import math
import jax
import jax.numpy as jnp
from jax import lax
from jax.sharding import PartitionSpec as P

DILATION_STEP = 2048


def shifted(value, axis, steps):
    count = lax.axis_size(axis)
    leading, last = (max(0, -steps), min(count, count - steps))
    return lax.ppermute(value, axis, [(source, source + steps) for source in range(leading, last)])


def contract_rows(left, right):
    return lax.dot_general(
        left, right, (((0,), (0,)), ((), ())), preferred_element_type=jnp.float32
    )


def gelu_parts(values):
    wide = values.astype(jnp.float32)
    cumul = 0.5 * (1.0 + jax.scipy.special.erf(wide / math.sqrt(2.0)))
    dense = jnp.exp(-0.5 * wide * wide) / math.sqrt(2.0 * math.pi)
    return (wide * cumul, cumul + wide * dense)


def shards(inputs, cotangent, conv_out, conv_weight, proj_weight):
    batches, sequence_length, chan_part = inputs.shape
    inner_width = conv_out.shape[2]
    row_count = batches * sequence_length
    flat_g = cotangent.reshape(row_count, chan_part)
    partial_mid = jnp.dot(flat_g, proj_weight.T, preferred_element_type=jnp.float32)
    summed_mid = lax.psum(partial_mid, "ch")
    middle_gradient = summed_mid.astype(jnp.bfloat16).reshape(batches, sequence_length, inner_width)
    neighbor_hops = DILATION_STEP // sequence_length
    following = shifted(middle_gradient, "seq", -neighbor_hops)
    preceding = shifted(middle_gradient, "seq", neighbor_hops)
    tap_list = (
        following.reshape(row_count, inner_width),
        middle_gradient.reshape(row_count, inner_width),
        preceding.reshape(row_count, inner_width),
    )
    grad_hidden = jnp.zeros((row_count, chan_part), jnp.float32)
    for tap_index in range(3):
        grad_hidden = grad_hidden + jnp.dot(
            tap_list[tap_index], conv_weight[tap_index].T, preferred_element_type=jnp.float32
        )
    hidden_full, deriv = gelu_parts(inputs.reshape(row_count, chan_part))
    hidden = hidden_full.astype(jnp.bfloat16)
    grad_inputs = (flat_g.astype(jnp.float32) + grad_hidden * deriv).astype(jnp.bfloat16)
    grad_inputs = grad_inputs.reshape(batches, sequence_length, chan_part)
    grad_scale = 1.0 / math.sqrt(float(row_count * lax.axis_size("seq")))
    conv_terms = jnp.stack(
        [contract_rows(hidden, tap_list[tap_index]) * grad_scale for tap_index in range(3)]
    )
    proj_terms = contract_rows(conv_out.reshape(row_count, inner_width), flat_g) * grad_scale
    conv_total, proj_total = lax.psum((conv_terms, proj_terms), "seq")
    return (grad_inputs, conv_total.astype(jnp.bfloat16), proj_total.astype(jnp.bfloat16))


def solution(mesh):
    in_specs = (
        P(None, "seq", "ch"),
        P(None, "seq", "ch"),
        P(None, "seq", None),
        P(None, "ch", None),
        P(None, "ch"),
    )
    out_specs = (P(None, "seq", "ch"), P(None, "ch", None), P(None, "ch"))
    return jax.shard_map(shards, mesh=mesh, in_specs=in_specs, out_specs=out_specs, check_vma=False)
```

profile of v0, /device:TPU:0, one launch (start us, length us, event | category | flops | bytes accessed | tf_op | source)
XLA Modules:
  0.0 702.9 jit_solution(10845579516698475319)
XLA Ops:
  0.6 0.0 copy-start
  0.6 7.7 %fusion.29 = f32[2048,768]{1,0:T(8,128)} fusion(bf16[2048,768]{1,0:T(8,128)(2,1)} %bitcast.60, bf16[768,768]{1,0:T(8,128)(2,1)} %param.9), kind=kOutput, calls=%fused_computation.36 | convolution fusion | flops 2415919104 | bytes 10616832 | tf_op jit(solution)/shard_map/dot_general | solution.py:34
  8.3 148.1 %all-reduce.3 = bf16[2048,768]{1,0:T(8,128)(2,1)} all-reduce(f32[2048,768]{1,0:T(8,128)} %fusion.29), channel_id=1, replica_groups=mesh['seq'=64,'ch'=2] {'ch'}, use_global_device_ids=true, to_apply=%region_0.0 | all-reduce | flops 1572864 | bytes 9437184 | tf_op jit(solution)/shard_map/psum | solution.py:35
  156.4 0.0 copy-start.3
  156.4 0.0 copy-start.5
  156.4 1.5 collective-permute-start
  157.9 6.3 collective-permute-start.1
  164.2 0.0 copy-done
  164.2 6.0 bitcast_multiply_fusion.2
  170.2 0.0 copy-done.3
  170.2 0.0 copy-done.5
  170.2 0.0 copy-start.2
  170.2 4.8 fusion.21
  175.0 0.0 copy-done.2
  175.0 1.6 fusion.10
  176.6 4.0 fusion.14
  180.6 2.7 multiply_bitcast_fusion
  183.3 112.8 %collective-permute-done = bf16[2,1024,768]{2,1,0:T(8,128)(2,1)S(1)} collective-permute-done((bf16[2,1024,768]{2,1,0:T(8,128)(2,1)}, bf16[2,1024,768]{2,1,0:T(8,128)(2,1)S(1)}, u32[]{:S(2)}, u32[]{:S(2)}) %collective-permute-start) | collective-permute-done | bytes 3145760 | tf_op jit(solution)/shard_map/ppermute | solution.py:13
  296.1 4.5 fusion.23
  300.6 2.7 fusion.16
  303.4 0.0 collective-permute-done.1
  303.4 0.0 copy-start.4
  303.4 1.6 copy-done.4
  305.0 2.7 fusion.15
  307.7 3.4 pad_maximum_fusion
  311.1 376.2 %all-reduce.4 = (bf16[3,768,768]{2,1,0:T(8,128)(2,1)}, bf16[768,768]{1,0:T(8,128)(2,1)}) all-reduce(f32[3,768,768]{2,1,0:T(8,128)} %pad_maximum_fusion, f32[768,768]{1,0:T(8,128)} %bitcast_multiply_fusion.2), channel_id=1, replica_groups=mesh['seq'=64,'ch'=2] {'seq'}, use_global_device_ids=true, to_apply=%region_1.0 | all-reduce | flops 2359296 | bytes 14155776 | tf_op jit(solution)/shard_map/psum | solution.py:59
  687.3 0.0 copy-start.1
  687.3 15.6 %fusion.6 = bf16[2048,768]{1,0:T(8,128)(2,1)} fusion(f32[2048,768]{1,0:T(8,128)} %get-tuple-element.6, bf16[2,1024,768]{2,1,0:T(8,128)(2,1)} %param.5, f32[2048,768]{1,0:T(8,128)} %fusion.23, f32[2048,768]{1,0:T(8,128)} %fusion.21, bf16[2048,768]{1,0:T(8,128)(2,1)} %bitcast.61, bf16[2048,768]{1,0:T(8,128)(2,1)} %bitcast.62, bf16[3,768,768]{2,1,0:T(8,128)(2,1)} %param.8), kind=kOutput, calls=%fused_computation.8 | convolution fusion | flops 2434793472 | bytes 32636928 | tf_op jit(solution)/shard_map/dot_general | solution.py:47
  702.9 0.0 copy-done.1
Async XLA Ops:
  0.6 163.6 %copy-start = (bf16[2,1024,768]{2,1,0:T(8,128)(2,1)S(1)}, bf16[2,1024,768]{2,1,0:T(8,128)(2,1)}, u32[]{:S(2)}) copy-start(bf16[2,1024,768]{2,1,0:T(8,128)(2,1)} %param.7) | copy-start | bytes 9437188
  156.4 13.8 %copy-start.3 = (bf16[2048,768]{1,0:T(8,128)(2,1)S(1)}, bf16[2048,768]{1,0:T(8,128)(2,1)}, u32[]{:S(2)}) copy-start(bf16[2048,768]{1,0:T(8,128)(2,1)} %all-reduce.3) | copy-start | bytes 9437188
  156.4 13.8 %copy-start.5 = (bf16[3,768,768]{2,1,0:T(8,128)(2,1)S(1)}, bf16[3,768,768]{2,1,0:T(8,128)(2,1)}, u32[]{:S(2)}) copy-start(bf16[3,768,768]{2,1,0:T(8,128)(2,1)} %param.8) | copy-start | bytes 10616836
  156.4 139.7 %collective-permute-start = (bf16[2,1024,768]{2,1,0:T(8,128)(2,1)}, bf16[2,1024,768]{2,1,0:T(8,128)(2,1)S(1)}, u32[]{:S(2)}, u32[]{:S(2)}) collective-permute-start(bf16[2,1024,768]{2,1,0:T(8,128)(2,1)} %bitcast.58), channel_id=1, source_target_pairs={{4,0},{6,2},{8,4},{10,6},{12,8},{14,10},{16,12},{18,14},{20,16},{2... | collective-permute-start | bytes 9437192 | tf_op jit(solution)/shard_map/ppermute | solution.py:13
  157.9 145.4 %collective-permute-start.1 = (bf16[2,1024,768]{2,1,0:T(8,128)(2,1)}, bf16[2,1024,768]{2,1,0:T(8,128)(2,1)S(1)}, u32[]{:S(2)}, u32[]{:S(2)}) collective-permute-start(bf16[2,1024,768]{2,1,0:T(8,128)(2,1)} %bitcast.59), channel_id=1, source_target_pairs={{0,4},{2,6},{4,8},{6,10},{8,12},{10,14},{12,16},{14,18},{16,20},{1... | collective-permute-start | bytes 9437192 | tf_op jit(solution)/shard_map/ppermute | solution.py:13
  170.2 4.8 copy-start.2
  303.4 1.6 copy-start.4
  687.3 15.6 %copy-start.1 = (bf16[2,1024,768]{2,1,0:T(8,128)(2,1)S(1)}, bf16[2,1024,768]{2,1,0:T(8,128)(2,1)}, u32[]{:S(2)}) copy-start(bf16[2,1024,768]{2,1,0:T(8,128)(2,1)} %param.7) | copy-start | bytes 9437188
where the time goes:
time: 703 us
  blocking collectives  524 us (75%)
  waiting for transfers between devices  113 us (16%)
  matrix products  46.7 us (7%)
  other arithmetic  8.96 us (1%)
  starting transfers between devices  7.8 us (1%)
    psum x1, blocking collectives, shards(): conv_total, proj_total = lax.psum((conv_terms, proj_terms), 'seq')  376 us
    psum x1, blocking collectives, shards(): summed_mid = lax.psum(partial_mid, 'ch')  148 us
    ppermute x2, waiting for transfers between devices, shifted(): lax.ppermute(value, axis, [(source, source + steps) for source in range(l...  113 us
    dot_general x3, matrix products, shards(): jnp.dot(tap_list[tap_index], conv_weight[tap_index].T, preferred_element_...  24.8 us
    dot_general x4, matrix products, contract_rows(): lax.dot_general(left, right, (((0,), (0,)), ((), ())), preferred_element_...  14.2 us
  transfers between devices with their start and end apart: 2, of which 1 were waited for; matrix products, arithmetic and copies ran while one was open for 4% of the time, Pallas kernels for 0%

commit v1 on v0

--- a/solution.py
+++ b/solution.py
@@ -32,7 +32,7 @@
     row_count = batches * sequence_length
     flat_g = cotangent.reshape(row_count, chan_part)
     partial_mid = jnp.dot(flat_g, proj_weight.T, preferred_element_type=jnp.float32)
-    summed_mid = lax.psum(partial_mid, "ch")
+    summed_mid = jnp.sum(lax.all_gather(partial_mid, "ch"), axis=0)
     middle_gradient = summed_mid.astype(jnp.bfloat16).reshape(batches, sequence_length, inner_width)
     neighbor_hops = DILATION_STEP // sequence_length
     following = shifted(middle_gradient, "seq", -neighbor_hops)

time: 703 us -> 736 us (1.047)
  waiting for transfers between devices: 113 us -> 271 us
  blocking collectives: 524 us -> 376 us
  between operations: 0.72 us -> 14.1 us
  other arithmetic: 8.96 us -> 19.3 us
    all_gather x0 -> x1, waiting for transfers between devices: none -> 158 us  [shards(): summed_mid = jnp.sum(lax.all_gather(partial_mid, 'ch'), axis=0)]
    psum x1 -> x0, blocking collectives: 148 us -> none  [shards(): summed_mid = lax.psum(partial_mid, 'ch')]
    reduce_sum x0 -> x1, other arithmetic: none -> 8.12 us  [shards(): summed_mid = jnp.sum(lax.all_gather(partial_mid, 'ch'), axis=0)]
  transfers between devices with their start and end apart: 2 -> 3, of which waited for: 1 -> 2; matrix products, arithmetic and copies ran while one was open for 4% -> 4% of each run, Pallas kernels for 0% -> 0%
where the time goes in v1:
time: 736 us; the launch traced here: 735 us
  blocking collectives  376 us (51%)
  waiting for transfers between devices  271 us (37%)
  matrix products  44.5 us (6%)
  other arithmetic  19.3 us (3%)
  between operations  14.1 us (2%)
  starting transfers between devices  7.78 us (1%)
    psum x1, blocking collectives, shards(): conv_total, proj_total = lax.psum((conv_terms, proj_terms), 'seq')  376 us
    all_gather x1, waiting for transfers between devices, shards(): summed_mid = jnp.sum(lax.all_gather(partial_mid, 'ch'), axis=0)  158 us
    ppermute x2, waiting for transfers between devices, shifted(): lax.ppermute(value, axis, [(source, source + steps) for source in range(l...  114 us
    dot_general x3, matrix products, shards(): jnp.dot(tap_list[tap_index], conv_weight[tap_index].T, preferred_element_...  24.6 us
  transfers between devices with their start and end apart: 3, of which 2 were waited for; matrix products, arithmetic and copies ran while one was open for 4% of the time, Pallas kernels for 0%

profile of v1, /device:TPU:0, one launch (start us, length us, event | category | flops | bytes accessed | tf_op | source)
XLA Modules:
  0.0 735.2 jit_solution(5325436519013255405)
XLA Ops:
  7.2 0.0 copy-start
  7.2 0.0 all-gather.3.cloned.1.call-start
  7.2 7.6 %fusion.29 = f32[2048,768]{1,0:T(8,128)} fusion(bf16[2048,768]{1,0:T(8,128)(2,1)} %bitcast.62, bf16[768,768]{1,0:T(8,128)(2,1)} %param.9), kind=kOutput, calls=%fused_computation.36 | convolution fusion | flops 2415919104 | bytes 10616832 | tf_op jit(solution)/shard_map/dot_general | solution.py:34
  14.8 0.0 all-gather.3.cloned.1.call-update
  14.9 157.7 %all-gather.3.cloned.1.call-done = f32[4096,768]{1,0:T(8,128)} async-done(((f32[2048,768]{1,0:T(8,128)}), f32[4096,768]{1,0:T(8,128)}) %all-gather.3.cloned.1.call-update) | async-done | bytes 12582928 | tf_op jit(solution)/shard_map/all_gather | solution.py:35
  172.5 8.1 %reduce_sum.9 = bf16[2048,768]{1,0:T(8,128)(2,1)} reduce(f32[2,2048,768]{2,1,0:T(8,128)} %bitcast.59, f32[]{:T(128)} %constant.2.clone.1), dimensions={0}, to_apply=%region_0.0 | reduce | flops 1572864 | bytes 15728644 | tf_op jit(solution)/shard_map/reduce_sum | solution.py:35
  180.7 0.0 copy-start.3
  180.7 0.0 copy-start.4
  180.7 1.5 collective-permute-start
  182.2 6.1 fusion.14
  188.4 0.0 copy-done.3
  188.4 0.0 copy-start.2
  188.4 6.2 collective-permute-start.1
  194.6 0.0 copy-done
  194.6 0.0 copy-done.4
  194.6 4.1 bitcast_multiply_fusion.2
  198.7 0.0 copy-done.2
  198.7 0.0 copy-start.7
  198.7 1.6 fusion.10
  200.4 0.4 copy-done.7
  200.7 4.5 fusion.21
  205.2 2.7 multiply_bitcast_fusion
  208.0 113.8 %collective-permute-done = bf16[2,1024,768]{2,1,0:T(8,128)(2,1)S(1)} collective-permute-done((bf16[2,1024,768]{2,1,0:T(8,128)(2,1)}, bf16[2,1024,768]{2,1,0:T(8,128)(2,1)S(1)}, u32[]{:S(2)}, u32[]{:S(2)}) %collective-permute-start) | collective-permute-done | bytes 3145760 | tf_op jit(solution)/shard_map/ppermute | solution.py:13
  321.8 4.5 fusion.23
  326.3 2.7 fusion.16
  329.0 0.0 collective-permute-done.1
  329.0 0.0 copy-start.5
  329.0 1.6 copy-done.5
  330.7 2.7 fusion.15
  333.4 0.0 copy-start.6
  333.4 3.4 pad_maximum_fusion
  336.8 0.0 copy-done.6
  336.8 376.0 %all-reduce.2 = (bf16[3,768,768]{2,1,0:T(8,128)(2,1)}, bf16[768,768]{1,0:T(8,128)(2,1)}) all-reduce(f32[3,768,768]{2,1,0:T(8,128)} %pad_maximum_fusion, f32[768,768]{1,0:T(8,128)S(1)} %copy-done.6), channel_id=1, replica_groups=mesh['seq'=64,'ch'=2] {'seq'}, use_global_device_ids=true, to_apply=%region_1.0 | all-reduce | flops 2359296 | bytes 14155776 | tf_op jit(solution)/shard_map/psum | solution.py:59
  712.8 0.0 copy-start.1
  712.8 15.6 %fusion.6 = bf16[2048,768]{1,0:T(8,128)(2,1)} fusion(f32[2048,768]{1,0:T(8,128)} %get-tuple-element.6, bf16[2,1024,768]{2,1,0:T(8,128)(2,1)} %param.5, f32[2048,768]{1,0:T(8,128)} %fusion.23, f32[2048,768]{1,0:T(8,128)} %fusion.21, bf16[2048,768]{1,0:T(8,128)(2,1)} %bitcast.63, bf16[2048,768]{1,0:T(8,128)(2,1)} %bitcast.64, bf16[3,768,768]{2,1,0:T(8,128)(2,1)} %param.8), kind=kOutput, calls=%fused_computation.8 | convolution fusion | flops 2434793472 | bytes 32636928 | tf_op jit(solution)/shard_map/dot_general | solution.py:47
  728.4 0.0 copy-done.1
Async XLA Ops:
  7.2 187.4 %copy-start = (bf16[2,1024,768]{2,1,0:T(8,128)(2,1)S(1)}, bf16[2,1024,768]{2,1,0:T(8,128)(2,1)}, u32[]{:S(2)}) copy-start(bf16[2,1024,768]{2,1,0:T(8,128)(2,1)} %param.7) | copy-start | bytes 9437188
  7.2 165.4 %all-gather.3.cloned.1.call-start = ((), (), s32[]{:S(2)}) async-start(), calls=%async_computation | async-start | bytes 18874368 | tf_op jit(solution)/shard_map/all_gather | solution.py:35
  180.7 7.7 %copy-start.3 = (bf16[2048,768]{1,0:T(8,128)(2,1)S(1)}, bf16[2048,768]{1,0:T(8,128)(2,1)}, u32[]{:S(2)}) copy-start(bf16[2048,768]{1,0:T(8,128)(2,1)} %reduce_sum.9) | copy-start | bytes 9437188
  180.7 13.9 %copy-start.4 = (bf16[2,1024,768]{2,1,0:T(8,128)(2,1)S(1)}, bf16[2,1024,768]{2,1,0:T(8,128)(2,1)}, u32[]{:S(2)}) copy-start(bf16[2,1024,768]{2,1,0:T(8,128)(2,1)} %param.6) | copy-start | bytes 9437188
  180.7 141.1 %collective-permute-start = (bf16[2,1024,768]{2,1,0:T(8,128)(2,1)}, bf16[2,1024,768]{2,1,0:T(8,128)(2,1)S(1)}, u32[]{:S(2)}, u32[]{:S(2)}) collective-permute-start(bf16[2,1024,768]{2,1,0:T(8,128)(2,1)} %bitcast.60), channel_id=1, source_target_pairs={{4,0},{6,2},{8,4},{10,6},{12,8},{14,10},{16,12},{18,14},{20,16},{2... | collective-permute-start | bytes 9437192 | tf_op jit(solution)/shard_map/ppermute | solution.py:13
  188.4 10.3 %copy-start.2 = (bf16[2,1024,768]{2,1,0:T(8,128)(2,1)S(1)}, bf16[2,1024,768]{2,1,0:T(8,128)(2,1)}, u32[]{:S(2)}) copy-start(bf16[2,1024,768]{2,1,0:T(8,128)(2,1)} %param.5) | copy-start | bytes 9437188
  188.4 140.7 %collective-permute-start.1 = (bf16[2,1024,768]{2,1,0:T(8,128)(2,1)S(1)}, bf16[2,1024,768]{2,1,0:T(8,128)(2,1)S(1)}, u32[]{:S(2)}, u32[]{:S(2)}) collective-permute-start(bf16[2,1024,768]{2,1,0:T(8,128)(2,1)S(1)} %bitcast.61), channel_id=1, source_target_pairs={{0,4},{2,6},{4,8},{6,10},{8,12},{10,14},{12,16},{14,18},{16,20},{1... | collective-permute-start | bytes 9437192 | tf_op jit(solution)/shard_map/ppermute | solution.py:13
  198.7 2.0 copy-start.7
  329.0 1.6 copy-start.5
  333.4 3.4 copy-start.6
  712.8 15.6 %copy-start.1 = (bf16[2,1024,768]{2,1,0:T(8,128)(2,1)S(1)}, bf16[2,1024,768]{2,1,0:T(8,128)(2,1)}, u32[]{:S(2)}) copy-start(bf16[2,1024,768]{2,1,0:T(8,128)(2,1)} %param.7) | copy-start | bytes 9437188
Sparse Core Ops, SparseCore 0:
  15.0 157.5 all-gather.2
